TPU v7x, 512 devices: a whole 4x8x8 slice. The times are simulated.
512 devices in a mesh: req: 128 (over z, y, core), tp: 4 (over x).
Axes of the slice: x: 4, y: 8, z: 8, core: 2. Of those that a mesh axis runs over, the one named last changes fastest.
Arguments:
- tokens: bfloat16 [49152, 3200], P('req'), may hold values from -6 to 6
- norm_gain: float32 [3200], replicated, may hold values from 0.5 to 2
- w_qkv: bfloat16 [3200, 6144], P('req', 'tp'), may hold values from -1 to 1
- q_gain: float32 [2048], P('tp'), may hold values from 0.5 to 2.5
- k_gain: float32 [2048], P('tp'), may hold values from 0.5 to 2.5
- w_out: bfloat16 [2048, 3200], P('tp', 'req'), may hold values from -0.125 to 0.125
- grids: int32 [384, 2], P('req'), may hold values from 2 to 16, as said below
- owners: int32 [12288], P('req'), may hold values from 0 to 127, as said below
- proj_gain: float32 [4, 3200], P(None, 'tp'), may hold values from 0.5 to 2
- proj_bias: float32 [4, 3200], P(None, 'tp'), may hold values from -3 to 3
Outputs:
- received: bfloat16 [32768, 4, 3200], P('req', None, 'tp')
Inputs may be any that keep to these rules, and one draw needn't show every extreme that they name: `grids`: each image spans at least 2 half grid rows. The images of one device together take at most 96 merged slots, and on one device in every draw exactly 96. `owners`: no device's merged slots, live or padding, name one owner more than 2 times; in every draw one owner is named exactly 2 times by every device.
All inputs are finite; a program needn't handle non-finite values.
Results may differ from a plain program's by a relative error of at most 0.009.
Values may be sent and summed in bfloat16 or wider, within the bound.
A program may use at most 128 MiB of HBM per device.

v0:
```python
import math
import jax
import jax.numpy as jnp
from jax import lax
from jax.sharding import PartitionSpec as P

D = 3200
HEADS = 16
HEAD_DIM = 128


def from_everyone(x, axis):
    copies = jnp.broadcast_to(x, (lax.axis_size(axis), *x.shape))
    return lax.all_to_all(copies, axis, split_axis=0, concat_axis=0, tiled=True)


def over_copies(x, axis):
    everything = from_everyone(x, axis)
    return jnp.sum(everything, axis=0)


def in_one(arrays, axis):
    ravelled, at, done = (jnp.concatenate([a.reshape(-1) for a in arrays]), 0, [])
    subtotal = over_copies(ravelled, axis)
    for a in arrays:
        done.append(subtotal[at : at + a.size].reshape(a.shape))
        at += a.size
    return tuple(done)


def merge_layout(grid, token_count, slot_count):
    half_rows = grid[:, 0]
    half_cols = grid[:, 1]
    image_slots = half_rows * half_cols
    slot_ends = jnp.cumsum(image_slots)
    slot_starts = slot_ends - image_slots
    slot_ids = jnp.arange(slot_count, dtype=jnp.int32)
    image_ids = jnp.sum((slot_ids[:, None] >= slot_ends[None, :]).astype(jnp.int32), axis=1)
    image_count = grid.shape[0]
    is_live = image_ids < image_count
    one_hot = (image_ids[:, None] == jnp.arange(image_count, dtype=jnp.int32)[None, :]).astype(
        jnp.int32
    )
    cols_here = jnp.maximum(jnp.sum(one_hot * half_cols[None, :], axis=1), 1)
    start_here = jnp.sum(one_hot * slot_starts[None, :], axis=1)
    offset = slot_ids - start_here
    row_half = offset // cols_here
    col_half = offset % cols_here
    first_row = 4 * start_here + 4 * row_half * cols_here + 2 * col_half
    patch_rows = jnp.stack(
        [first_row, first_row + 1, first_row + 2 * cols_here, first_row + 2 * cols_here + 1], axis=1
    )
    patch_rows = jnp.where(is_live[:, None], patch_rows, 0)
    token_ids = jnp.arange(token_count, dtype=jnp.int32)
    segment = jnp.sum((token_ids[:, None] >= 4 * slot_ends[None, :]).astype(jnp.int32), axis=1)
    return (patch_rows, is_live, segment)


def owner_ranks(owner_ids, is_live):
    slot_ids = jnp.arange(owner_ids.shape[0], dtype=jnp.int32)
    earlier = (
        (owner_ids[:, None] == owner_ids[None, :])
        & (slot_ids[None, :] < slot_ids[:, None])
        & is_live[None, :]
    )
    return jnp.sum(earlier.astype(jnp.int32), axis=1)


def body(tokens, norm_gain, w_qkv, q_gain, k_gain, w_out, grids, owners, proj_gain, proj_bias):
    token_count = tokens.shape[0]
    slot_count = owners.shape[0]
    quarter = proj_gain.shape[1]
    head_share = q_gain.shape[0]
    head_count = head_share // HEAD_DIM
    head_width = HEADS * HEAD_DIM
    score_scale = 1.0 / math.sqrt(HEAD_DIM)
    feature_total = 4 * D
    devices_req = lax.axis_size("req")
    capacity = max(2, (2 * slot_count + devices_req - 1) // devices_req)
    patch_rows, is_live, segment = merge_layout(grids, token_count, slot_count)
    token_float = tokens.astype(jnp.float32)
    mean_square = jnp.mean(token_float * token_float, axis=1, keepdims=True)
    normed = (token_float * lax.rsqrt(mean_square + 1e-06) * norm_gain).astype(jnp.bfloat16)
    projected = jnp.dot(
        normed, lax.all_gather(w_qkv, "req", axis=0, tiled=True), preferred_element_type=jnp.float32
    )
    projected = projected.reshape(token_count, head_count, 3, HEAD_DIM)
    queries = projected[:, :, 0]
    key_vecs = projected[:, :, 1]
    values = projected[:, :, 2].astype(jnp.bfloat16)
    q_gains = q_gain.reshape(head_count, HEAD_DIM)
    k_gains = k_gain.reshape(head_count, HEAD_DIM)
    local_q = jnp.sum(queries * queries, axis=(1, 2))
    local_k = jnp.sum(key_vecs * key_vecs, axis=(1, 2))
    q_total, k_total = in_one((local_q, local_k), "tp")
    q_scale = lax.rsqrt(q_total / head_width + 1e-06)
    k_scale = lax.rsqrt(k_total / head_width + 1e-06)
    q_normed = queries * q_scale[:, None, None] * q_gains
    k_normed = key_vecs * k_scale[:, None, None] * k_gains
    scores = (
        jnp.einsum("qhd,khd->hqk", q_normed, k_normed, precision=lax.Precision.HIGHEST)
        * score_scale
    )
    same_image = segment[:, None] == segment[None, :]
    scores = jnp.where(same_image[None], scores, -1e30)
    row_top = jnp.max(scores, axis=2, keepdims=True)
    weights_raw = jnp.exp(scores - row_top)
    probs = (weights_raw / jnp.sum(weights_raw, axis=2, keepdims=True)).astype(jnp.bfloat16)
    attended = jnp.einsum("hqk,khd->qhd", probs, values, preferred_element_type=jnp.float32)
    attended = attended.astype(jnp.bfloat16).reshape(token_count, head_share)
    partial_sum = jnp.dot(
        attended,
        lax.all_gather(w_out, "req", axis=1, tiled=True),
        preferred_element_type=jnp.float32,
    )
    mine = lax.psum_scatter(
        partial_sum.astype(jnp.bfloat16), "tp", scatter_dimension=1, tiled=True
    ).astype(jnp.float32)
    token_mine = lax.dynamic_slice_in_dim(token_float, lax.axis_index("tp") * quarter, quarter, 1)
    hidden = (token_mine + mine).astype(jnp.bfloat16)
    merged = jnp.where(is_live[:, None, None], hidden[patch_rows], jnp.zeros((), jnp.bfloat16))
    ranks = owner_ranks(owners, is_live)
    target_owner = jnp.where(is_live, owners, devices_req)
    merged_float = merged.astype(jnp.float32)
    row_sum = jnp.sum(merged_float, axis=(1, 2))
    row_sq = jnp.sum(merged_float * merged_float, axis=(1, 2))
    row_sum, row_sq = in_one((row_sum, row_sq), "tp")
    mean_value = row_sum / feature_total
    variance = row_sq / feature_total - mean_value * mean_value
    normed_rows = (merged_float - mean_value[:, None, None]) * lax.rsqrt(variance + 1e-05)[
        :, None, None
    ] * proj_gain + proj_bias
    normed_rows = jnp.where(is_live[:, None, None], normed_rows, 0.0).astype(jnp.bfloat16)
    send_slots = jnp.zeros((devices_req, capacity, 4, quarter), jnp.bfloat16)
    send_slots = send_slots.at[target_owner, ranks].set(normed_rows, mode="drop")
    arrived = lax.all_to_all(send_slots, "req", split_axis=0, concat_axis=0, tiled=True)
    result = arrived.reshape(devices_req * capacity, 4, quarter)
    return result


def solution(mesh):
    placed = (
        P("req", None),
        P(),
        P("req", "tp"),
        P("tp"),
        P("tp"),
        P("tp", "req"),
        P("req", None),
        P("req"),
        P(None, "tp"),
        P(None, "tp"),
    )
    return jax.shard_map(
        body, mesh=mesh, in_specs=placed, out_specs=P("req", None, "tp"), check_vma=False
    )
```

profile of v0, /device:TPU:8, one launch (start us, length us, event | category | flops | bytes accessed | tf_op | source)
XLA Modules:
  0.0 339.7 jit_solution(6515635948324033190)
XLA Ops:
  6.5 0.0 all-gather.5.cloned.1.call-start
  6.5 0.7 all-gather.5.cloned.1.call-update
  7.3 0.0 all-gather.7.cloned.1.call-start
  7.3 0.7 all-gather.7.cloned.1.call-update
  8.0 0.0 copy-start.5
  8.0 4.2 %copy.44 = bf16[384,3200]{0,1:T(8,128)(2,1)S(1)} copy(bf16[384,3200]{1,0:T(8,128)(2,1)} %param.10) | data formatting | bytes 4915200 | tf_op args[0]
  12.3 0.0 copy-done.5
  12.3 0.2 reduce-window.7
  12.5 0.1 convert_reduce_fusion.2
  12.5 0.6 multiply_reduce_fusion
  13.2 92.8 %all-gather.5.cloned.1.call-done = bf16[128,25,1536]{2,1,0:T(8,128)(2,1)} async-done(((bf16[1,25,1536]{2,1,0:T(8,128)(2,1)}), bf16[128,25,1536]{2,1,0:T(8,128)(2,1)}) %all-gather.5.cloned.1.call-update) | async-done | bytes 9830416 | tf_op jit(solution)/shard_map/all_gather | solution.py:85
  105.9 14.4 %reshape.394 = bf16[3200,1536]{1,0:T(8,128)(2,1)} reshape(bf16[128,25,1536]{2,1,0:T(8,128)(2,1)} %all-gather.5.cloned.1.call-done) | data formatting | bytes 19660800
  120.3 0.0 copy-done.8
  120.3 8.5 %fusion.1 = f32[384,1536]{0,1:T(8,128)S(1)} fusion(bf16[3200,1536]{1,0:T(8,128)(2,1)} %reshape.394, f32[3200]{0:T(1024)S(1)} %copy-done.8, f32[384]{0:T(512)S(1)} %add_rsqrt_fusion.2, bf16[384,3200]{0,1:T(8,128)(2,1)S(1)} %copy.44), kind=kOutput, calls=%fused_computation.6 | convolution fusion | flops 3779788800 | bytes 14661632 | tf_op jit(solution)/shard_map/dot_general | solution.py:84
  128.8 0.0 copy-start
  128.8 1.4 copy-done
  130.2 0.1 multiply_reduce_fusion.2
  130.4 0.6 broadcast_in_dim.61
  131.0 4.2 %all-to-all-start = ((f32[4,1,768]{2,1,0:T(1,128)}), f32[4,1,768]{2,1,0:T(1,128)S(1)}, u32[]{:S(2)}, u32[]{:S(2)}) async-start(f32[4,1,768]{2,1,0:T(1,128)} %broadcast_in_dim.61), calls=%async_computation | async-start | bytes 24576 | tf_op jit(solution)/shard_map/all_to_all | solution.py:14
  135.2 0.0 reduce-scatter.2.cloned.1.call-start
  135.2 0.1 broadcast_compare_fusion
  135.4 0.0 copy-start.6
  135.4 0.0 copy-start.7
  135.4 54.9 %all-gather.7.cloned.1.call-done = bf16[128,25,512]{2,1,0:T(8,128)(2,1)} async-done(((bf16[1,25,512]{2,1,0:T(8,128)(2,1)}), bf16[128,25,512]{2,1,0:T(8,128)(2,1)}) %all-gather.7.cloned.1.call-update) | async-done | bytes 3276816 | tf_op jit(solution)/shard_map/all_gather | solution.py:113
  190.3 5.8 %reshape.396 = bf16[3200,512]{1,0:T(8,128)(2,1)} reshape(bf16[128,25,512]{2,1,0:T(8,128)(2,1)} %all-gather.7.cloned.1.call-done) | data formatting | bytes 6553600
  196.1 0.0 all-to-all-done
  196.1 0.0 copy-done.6
  196.1 0.0 copy-done.7
  196.2 3.7 %fusion.15 = f32[4,384,384]{1,2,0:T(8,128)S(1)} fusion(f32[384,4,3,128]{0,3,2,1:T(8,128)} %bitcast.115, f32[4,128]{1,0:T(4,128)S(1)} %bitcast.119, f32[384]{0:T(512)S(1)} %get-tuple-element.13, f32[4,128]{1,0:T(4,128)S(1)} %bitcast.120, f32[384]{0:T(512)S(1)} %get-tuple-element.12), kind=kOutput, calls=%fused_computation.31 | convolution fusion | flops 906756096 | bytes 3939328 | tf_op jit(solution)/shard_map/qhd,khd->hqk/dot_general | solution.py:101
  199.8 0.0 copy-start.1
  199.8 1.4 copy-done.1
  201.2 0.8 fusion.44
  202.0 2.9 convolution_convert_fusion.1
  204.9 5.3 %convolution_convert_fusion = bf16[384,3200]{0,1:T(8,128)(2,1)} fusion(bf16[3200,512]{1,0:T(8,128)(2,1)} %reshape.396, bf16[384,512]{0,1:T(8,128)(2,1)S(1)} %bitcast.122), kind=kOutput, calls=%fused_computation.3 | convolution fusion | flops 1259520000 | bytes 6127616 | tf_op jit(solution)/shard_map/dot_general | solution.py:111
  210.2 0.0 reduce-scatter.2.cloned.1.call-update
  210.2 0.0 copy-start.4
  210.2 2.5 convert_element_type.46
  212.7 0.1 convert_reduce_fusion.3
  212.8 0.1 select_reduce_fusion.1
  212.9 0.1 fusion.43
  213.1 0.1 copy.51
  213.2 0.1 reshape.380
  213.3 0.0 copy-done.4
  213.3 0.2 convert_reduce_fusion.1
  213.5 32.1 %reduce-scatter.2.cloned.1.call-done = bf16[384,800]{0,1:T(8,128)(2,1)} async-done(((bf16[384,3200]{0,1:T(8,128)(2,1)}), bf16[384,800]{0,1:T(8,128)(2,1)}) %reduce-scatter.2.cloned.1.call-update) | async-done | bytes 614416 | tf_op jit(solution)/shard_map/reduce_scatter | solution.py:116
  245.6 1.6 add_convert_fusion
  247.2 0.3 copy.52
  247.5 2.3 gather_fusion
  249.8 0.0 copy-start.2
  249.8 0.0 copy-start.3
  249.9 0.2 reshape.379
  250.0 1.7 convert_reduce_fusion
  251.7 0.1 pad_maximum_fusion.1
  251.8 0.6 broadcast_in_dim.104
  252.4 3.2 all-to-all-start.1
  255.6 5.2 %all-to-all-done.1 = f32[4,1,192]{2,1,0:T(1,128)S(1)} async-done(((f32[4,1,192]{2,1,0:T(1,128)}), f32[4,1,192]{2,1,0:T(1,128)S(1)}, u32[]{:S(2)}, u32[]{:S(2)}) %all-to-all-start.1) | async-done | bytes 3104 | tf_op jit(solution)/shard_map/all_to_all | solution.py:14
  260.9 0.1 slice_multiply_fusion
  261.0 0.0 copy-done.2
  261.0 0.0 copy-done.3
  261.0 0.7 fusion.11
  261.7 0.5 broadcast_in_dim.56
  262.2 4.6 %scatter_fusion = bf16[128,2,4,800]{3,2,1,0:T(4,128)(2,1)S(1)} fusion(bf16[128,2,4,800]{3,2,1,0:T(4,128)(2,1)S(1)} %broadcast_in_dim.56, s32[96]{0:T(128)S(1)} %fusion.34, bf16[96,4,800]{2,1,0:T(4,128)(2,1)S(1)} %fusion.11), kind=kCustom, calls=%fused_computation.1 | custom fusion | bytes 1843968 | tf_op jit(solution)/shard_map/scatter | solution.py:135
  266.8 62.3 %all_to_all.17 = bf16[128,2,4,800]{3,2,1,0:T(4,128)(2,1)} all-to-all(bf16[128,2,4,800]{3,2,1,0:T(4,128)(2,1)S(1)} %scatter_fusion), channel_id=1, replica_groups=mesh['req'=128,'tp'=4] {'req'}, dimensions={0} | all-to-all | bytes 3276800 | tf_op jit(solution)/shard_map/all_to_all | solution.py:136
  329.2 4.0 %copy.54 = bf16[256,4,800]{0,2,1:T(8,128)(2,1)} copy(bf16[256,4,800]{2,1,0:T(4,128)(2,1)} %bitcast.113) | data formatting | bytes 3276800 | tf_op jit(solution)/shard_map/reshape | solution.py:137
  (12 shorter events, 0.1 us)
Async XLA Ops:
  6.5 99.4 %all-gather.5.cloned.1.call-start = ((), (), s32[]{:S(2)}) async-start(), calls=%async_computation.5 | async-start | bytes 12681216 | tf_op jit(solution)/shard_map/all_gather | solution.py:85
  7.3 183.0 %all-gather.7.cloned.1.call-start = ((), (), s32[]{:S(2)}) async-start(), calls=%async_computation.6 | async-start | bytes 4227072 | tf_op jit(solution)/shard_map/all_gather | solution.py:113
  8.0 4.2 %copy-start.5 = (s32[3,2]{0,1:T(2,128)S(1)}, s32[3,2]{0,1:T(2,128)}, u32[]{:S(2)}) copy-start(s32[3,2]{0,1:T(2,128)} %param.16) | copy-start | bytes 76
  13.2 107.1 %copy-start.8 = (f32[3200]{0:T(1024)S(1)}, f32[3200]{0:T(1024)}, u32[]{:S(2)}) copy-start(f32[3200]{0:T(1024)} %param.11) | copy-start | bytes 38404
  128.8 1.5 copy-start
  131.0 65.1 %all-to-all-start = ((f32[4,1,768]{2,1,0:T(1,128)}), f32[4,1,768]{2,1,0:T(1,128)S(1)}, u32[]{:S(2)}, u32[]{:S(2)}) async-start(f32[4,1,768]{2,1,0:T(1,128)} %broadcast_in_dim.61), calls=%async_computation | async-start | bytes 24576 | tf_op jit(solution)/shard_map/all_to_all | solution.py:14
  135.2 110.4 %reduce-scatter.2.cloned.1.call-start = ((), (), s32[]{:S(2)}) async-start(), calls=%async_computation.4 | async-start | bytes 3072000 | tf_op jit(solution)/shard_map/reduce_scatter | solution.py:116
  135.4 60.8 %copy-start.6 = (f32[512]{0:T(512)S(1)}, f32[512]{0:T(512)}, u32[]{:S(2)}) copy-start(f32[512]{0:T(512)} %param.14) | copy-start | bytes 6148
  135.4 60.8 %copy-start.7 = (f32[512]{0:T(512)S(1)}, f32[512]{0:T(512)}, u32[]{:S(2)}) copy-start(f32[512]{0:T(512)} %param.13) | copy-start | bytes 6148
  199.8 1.4 copy-start.1
  210.2 3.1 copy-start.4
  249.8 11.2 %copy-start.2 = (f32[4,800]{1,0:T(4,128)S(1)}, f32[4,800]{1,0:T(4,128)}, u32[]{:S(2)}) copy-start(f32[4,800]{1,0:T(4,128)} %param.19) | copy-start | bytes 38404
  249.8 11.1 %copy-start.3 = (f32[4,800]{1,0:T(4,128)S(1)}, f32[4,800]{1,0:T(4,128)}, u32[]{:S(2)}) copy-start(f32[4,800]{1,0:T(4,128)} %param.18) | copy-start | bytes 38404
  252.4 8.5 %all-to-all-start.1 = ((f32[4,1,192]{2,1,0:T(1,128)}), f32[4,1,192]{2,1,0:T(1,128)S(1)}, u32[]{:S(2)}, u32[]{:S(2)}) async-start(f32[4,1,192]{2,1,0:T(1,128)} %broadcast_in_dim.104), calls=%async_computation.2 | async-start | bytes 8192 | tf_op jit(solution)/shard_map/all_to_all | solution.py:14
Sparse Core Ops, SparseCore 0:
  10.5 95.4 all-gather.4
  109.1 81.1 all-gather.6
  210.3 35.2 reduce-scatter.1
where the time goes:
time: 341 us; the launch traced here: 340 us
  waiting for transfers between devices  186 us (55%)
  blocking collectives  62.3 us (18%)
  local copies, waits for them, and re-layouts  40.6 us (12%)
  matrix products  20.3 us (6%)
  between operations  13.4 us (4%)
  other arithmetic  9.19 us (3%)
  starting transfers between devices  7.54 us (2%)
    all_gather x1, waiting for transfers between devices, body(): lax.all_gather(w_qkv, 'req', axis=0, tiled=True)  92.8 us
    all_to_all x1, blocking collectives, body(): lax.all_to_all(send_slots, 'req', split_axis=0, concat_axis=0, tiled=True)  62.3 us
    all_gather x1, waiting for transfers between devices, body(): lax.all_gather(w_out, 'req', axis=1, tiled=True)  54.9 us
    reduce_scatter x1, waiting for transfers between devices, body(): lax.psum_scatter(partial_sum.astype(jnp.bfloat16), 'tp', scatter_dimensio...  32.1 us
    unnamed x21, local copies, waits for them, and re-layouts  27.3 us
    dot_general x1, matrix products, body(): jnp.dot(normed, lax.all_gather(w_qkv, 'req', axis=0, tiled=True), preferr...  8.45 us
    all_to_all x2, starting transfers between devices, from_everyone(): return lax.all_to_all(copies, axis, split_axis=0, concat_axis=0, tiled=True)  7.49 us
  transfers between devices with their start and end apart: 5, of which 4 were waited for; matrix products, arithmetic and copies ran while one was open for 11% of the time, Pallas kernels for 0%

commit v1 on v0

--- a/solution.py
+++ b/solution.py
@@ -82,7 +82,11 @@
     mean_square = jnp.mean(token_float * token_float, axis=1, keepdims=True)
     normed = (token_float * lax.rsqrt(mean_square + 1e-06) * norm_gain).astype(jnp.bfloat16)
     projected = jnp.dot(
-        normed, lax.all_gather(w_qkv, "req", axis=0, tiled=True), preferred_element_type=jnp.float32
+        normed,
+        jnp.concatenate(
+            lax.all_to_all(jnp.stack([w_qkv] * lax.axis_size("req")), "req", 0, 0), axis=0
+        ),
+        preferred_element_type=jnp.float32,
     )
     projected = projected.reshape(token_count, head_count, 3, HEAD_DIM)
     queries = projected[:, :, 0]

time: 341 us -> 649 us (1.90)
  waiting for transfers between devices: 186 us -> 457 us
  local copies, waits for them, and re-layouts: 40.6 us -> 60.5 us
  starting transfers between devices: 7.54 us -> 24.5 us
    all_to_all x0 -> x1, waiting for transfers between devices: none -> 382 us  [body(): lax.all_to_all(jnp.stack([w_qkv] * lax.axis_size('req')), 'req', 0, 0)]
    all_gather x1 -> x0, waiting for transfers between devices: 92.8 us -> none  [body(): lax.all_gather(w_qkv, 'req', axis=0, tiled=True)]
    all_gather x1, waiting for transfers between devices: 54.9 us -> 0.02 us  [body(): lax.all_gather(w_out, 'req', axis=1, tiled=True)]
    reduce_scatter x1, waiting for transfers between devices: 32.1 us -> 69.1 us  [body(): lax.psum_scatter(partial_sum.astype(jnp.bfloat16), 'tp', scatter_dimensio...]
    all_to_all x0 -> x1, starting transfers between devices: none -> 17.8 us  [body(): lax.all_to_all(jnp.stack([w_qkv] * lax.axis_size('req')), 'req', 0, 0)]
    reshape x0 -> x1, local copies, waits for them, and re-layouts: none -> 14.4 us  [body(): jnp.concatenate(lax.all_to_all(jnp.stack([w_qkv] * lax.axis_size('req')),...]
    unnamed x21 -> x20, local copies, waits for them, and re-layouts: 27.3 us -> 12.9 us
    dot_general x0 -> x1, local copies, waits for them, and re-layouts: none -> 13 us  [body(): jnp.dot(normed, jnp.concatenate(lax.all_to_all(jnp.stack([w_qkv] * lax.ax...]
  transfers between devices with their start and end apart: 5 -> 5, of which waited for: 4 -> 3; matrix products, arithmetic and copies ran while one was open for 11% -> 8% of each run, Pallas kernels for 0% -> 0%
where the time goes in v1:
time: 649 us; the launch traced here: 648 us
  waiting for transfers between devices  457 us (70%)
  blocking collectives  62.3 us (10%)
  local copies, waits for them, and re-layouts  60.5 us (9%)
  starting transfers between devices  24.5 us (4%)
  matrix products  19.9 us (3%)
  between operations  13.7 us (2%)
  other arithmetic  9.19 us (1%)
    all_to_all x1, waiting for transfers between devices, body(): lax.all_to_all(jnp.stack([w_qkv] * lax.axis_size('req')), 'req', 0, 0)  382 us
    reduce_scatter x1, waiting for transfers between devices, body(): lax.psum_scatter(partial_sum.astype(jnp.bfloat16), 'tp', scatter_dimensio...  69.1 us
    all_to_all x1, blocking collectives, body(): lax.all_to_all(send_slots, 'req', split_axis=0, concat_axis=0, tiled=True)  62.3 us
    all_to_all x1, starting transfers between devices, body(): lax.all_to_all(jnp.stack([w_qkv] * lax.axis_size('req')), 'req', 0, 0)  17.8 us
    reshape x1, local copies, waits for them, and re-layouts, body(): jnp.concatenate(lax.all_to_all(jnp.stack([w_qkv] * lax.axis_size('req')),...  14.4 us
    dot_general x1, local copies, waits for them, and re-layouts, body(): jnp.dot(normed, jnp.concatenate(lax.all_to_all(jnp.stack([w_qkv] * lax.ax...  13 us
  transfers between devices with their start and end apart: 5, of which 3 were waited for; matrix products, arithmetic and copies ran while one was open for 8% of the time, Pallas kernels for 0%

profile of v1, /device:TPU:8, one launch (start us, length us, event | category | flops | bytes accessed | tf_op | source)
XLA Modules:
  0.0 647.6 jit_solution(15044792731155251491)
XLA Ops:
  6.5 6.9 %stack.12 = bf16[128,25,1536]{2,1,0:T(8,128)(2,1)} broadcast(bf16[25,1536]{1,0:T(8,128)(2,1)} %param.12), dimensions={1,2} | broadcast | bytes 9907200 | tf_op jit(solution)/shard_map/stack | solution.py:87
  13.5 17.8 %all-to-all-start = ((bf16[128,25,1536]{2,1,0:T(8,128)(2,1)}), bf16[128,25,1536]{2,1,0:T(8,128)(2,1)}, u32[]{:S(2)}, u32[]{:S(2)}) async-start(bf16[128,25,1536]{2,1,0:T(8,128)(2,1)} %stack.12), calls=%async_computation | async-start | bytes 25165824 | tf_op jit(solution)/shard_map/all_to_all | solution.py:87
  31.2 0.0 all-gather.3.cloned.1.call-start
  31.3 0.7 all-gather.3.cloned.1.call-update
  32.0 0.0 copy-start.5
  32.0 4.2 copy.45
  36.2 0.0 copy-done.5
  36.2 0.2 reduce-window.7
  36.4 0.1 convert_reduce_fusion.2
  36.5 0.6 multiply_reduce_fusion
  37.1 382.4 %all-to-all-done = bf16[128,25,1536]{2,1,0:T(8,128)(2,1)} async-done(((bf16[128,25,1536]{2,1,0:T(8,128)(2,1)}), bf16[128,25,1536]{2,1,0:T(8,128)(2,1)}, u32[]{:S(2)}, u32[]{:S(2)}) %all-to-all-start) | async-done | bytes 9830432 | tf_op jit(solution)/shard_map/all_to_all | solution.py:87
  419.6 14.4 %reshape.379 = bf16[3200,1536]{1,0:T(8,128)(2,1)} reshape(bf16[128,25,1536]{2,1,0:T(8,128)(2,1)} %all-to-all-done) | data formatting | bytes 19660800 | tf_op jit(solution)/shard_map/reshape | solution.py:86
  433.9 13.0 %copy.46 = bf16[1536,3200]{1,0:T(8,128)(2,1)} copy(bf16[1536,3200]{0,1:T(8,128)(2,1)} %bitcast.115) | data formatting | bytes 19660800 | tf_op jit(solution)/shard_map/dot_general | solution.py:84
  446.9 0.0 copy-done.8
  446.9 8.1 %fusion.2 = f32[384,4,3,128]{0,3,2,1:T(8,128)S(1)} fusion(bf16[4,3,128,3200]{3,2,1,0:T(8,128)(2,1)} %bitcast.116, f32[3200]{0:T(1024)S(1)} %copy-done.8, f32[384]{0:T(512)S(1)} %add_rsqrt_fusion.2, bf16[384,3200]{0,1:T(8,128)(2,1)S(1)} %copy.45), kind=kOutput, calls=%fused_computation.7 | convolution fusion | flops 3779788800 | bytes 14661632 | tf_op jit(solution)/shard_map/dot_general | solution.py:84
  455.0 0.0 copy-start
  455.0 1.4 copy-done
  456.5 0.1 multiply_reduce_fusion.2
  456.6 0.6 broadcast_in_dim.61
  457.2 3.3 all-to-all-start.1
  460.5 0.2 reduce-scatter.2.cloned.1.call-start
  460.7 0.1 broadcast_compare_fusion
  460.9 0.0 copy-start.6
  460.9 0.0 copy-start.7
  460.9 0.0 all-gather.3.cloned.1.call-done
  460.9 5.8 reshape.398
  466.8 0.0 all-to-all-done.1
  466.8 0.0 copy-done.6
  466.8 0.0 copy-done.7
  466.8 3.7 fusion.17
  470.5 0.0 copy-start.1
  470.5 1.4 copy-done.1
  471.9 0.8 fusion.46
  472.6 2.9 convolution_convert_fusion.1
  475.6 5.3 convolution_convert_fusion
  480.8 0.0 reduce-scatter.2.cloned.1.call-update
  480.9 0.0 copy-start.4
  480.9 2.5 convert_element_type.46
  483.4 0.1 convert_reduce_fusion.3
  483.5 0.1 select_reduce_fusion.1
  483.6 0.1 fusion.45
  483.7 0.1 copy.52
  483.8 0.1 reshape.384
  484.0 0.0 copy-done.4
  484.0 0.2 convert_reduce_fusion.1
  484.1 69.1 %reduce-scatter.2.cloned.1.call-done = bf16[384,800]{0,1:T(8,128)(2,1)} async-done(((bf16[384,3200]{0,1:T(8,128)(2,1)}), bf16[384,800]{0,1:T(8,128)(2,1)}) %reduce-scatter.2.cloned.1.call-update) | async-done | bytes 614416 | tf_op jit(solution)/shard_map/reduce_scatter | solution.py:120
  553.2 1.6 add_convert_fusion
  554.8 0.3 copy.53
  555.2 2.3 gather_fusion
  557.5 0.0 copy-start.2
  557.5 0.0 copy-start.3
  557.5 0.2 reshape.383
  557.7 1.7 convert_reduce_fusion
  559.3 0.1 pad_maximum_fusion.1
  559.4 0.6 broadcast_in_dim.104
  560.0 3.2 all-to-all-start.2
  563.3 5.2 all-to-all-done.2
  568.5 0.1 slice_multiply_fusion
  568.6 0.0 copy-done.2
  568.6 0.7 fusion.13
  569.4 0.5 broadcast_in_dim.56
  569.9 4.6 scatter_fusion
  574.4 62.3 %all_to_all.22 = bf16[128,2,4,800]{3,2,1,0:T(4,128)(2,1)} all-to-all(bf16[128,2,4,800]{3,2,1,0:T(4,128)(2,1)S(1)} %scatter_fusion), channel_id=1, replica_groups=mesh['req'=128,'tp'=4] {'req'}, dimensions={0} | all-to-all | bytes 3276800 | tf_op jit(solution)/shard_map/all_to_all | solution.py:140
  636.7 4.0 copy.55
  (13 shorter events, 0.1 us)
Async XLA Ops:
  13.5 406.1 %all-to-all-start = ((bf16[128,25,1536]{2,1,0:T(8,128)(2,1)}), bf16[128,25,1536]{2,1,0:T(8,128)(2,1)}, u32[]{:S(2)}, u32[]{:S(2)}) async-start(bf16[128,25,1536]{2,1,0:T(8,128)(2,1)} %stack.12), calls=%async_computation | async-start | bytes 25165824 | tf_op jit(solution)/shard_map/all_to_all | solution.py:87
  31.2 429.7 %all-gather.3.cloned.1.call-start = ((), (), s32[]{:S(2)}) async-start(), calls=%async_computation.6 | async-start | bytes 4227072 | tf_op jit(solution)/shard_map/all_gather | solution.py:117
  32.0 4.2 copy-start.5
  433.9 13.0 %copy-start.8 = (f32[3200]{0:T(1024)S(1)}, f32[3200]{0:T(1024)}, u32[]{:S(2)}) copy-start(f32[3200]{0:T(1024)} %param.11) | copy-start | bytes 38404
  455.0 1.5 copy-start
  457.2 9.5 %all-to-all-start.1 = ((f32[4,1,768]{2,1,0:T(1,128)}), f32[4,1,768]{2,1,0:T(1,128)S(1)}, u32[]{:S(2)}, u32[]{:S(2)}) async-start(f32[4,1,768]{2,1,0:T(1,128)} %broadcast_in_dim.61), calls=%async_computation.1 | async-start | bytes 24576 | tf_op jit(solution)/shard_map/all_to_all | solution.py:14
  460.5 92.7 %reduce-scatter.2.cloned.1.call-start = ((), (), s32[]{:S(2)}) async-start(), calls=%async_computation.5 | async-start | bytes 3072000 | tf_op jit(solution)/shard_map/reduce_scatter | solution.py:120
  460.9 5.9 copy-start.6
  460.9 5.9 copy-start.7
  470.5 1.4 copy-start.1
  480.9 3.1 copy-start.4
  557.5 11.2 %copy-start.2 = (f32[4,800]{1,0:T(4,128)S(1)}, f32[4,800]{1,0:T(4,128)}, u32[]{:S(2)}) copy-start(f32[4,800]{1,0:T(4,128)} %param.19) | copy-start | bytes 38404
  557.5 11.1 %copy-start.3 = (f32[4,800]{1,0:T(4,128)S(1)}, f32[4,800]{1,0:T(4,128)}, u32[]{:S(2)}) copy-start(f32[4,800]{1,0:T(4,128)} %param.18) | copy-start | bytes 38404
  560.0 8.5 %all-to-all-start.2 = ((f32[4,1,192]{2,1,0:T(1,128)}), f32[4,1,192]{2,1,0:T(1,128)S(1)}, u32[]{:S(2)}, u32[]{:S(2)}) async-start(f32[4,1,192]{2,1,0:T(1,128)} %broadcast_in_dim.104), calls=%async_computation.3 | async-start | bytes 8192 | tf_op jit(solution)/shard_map/all_to_all | solution.py:14
Sparse Core Ops, SparseCore 0:
  35.2 373.5 all-gather.2
  481.0 72.1 reduce-scatter.1
